TPU v7x, 32 devices: a whole 2x2x4 slice. The times are simulated.
32 devices in a mesh: orig: 8 (over z, core), dest: 4 (over y, x).
Axes of the slice: x: 2, y: 2, z: 4, core: 2. Of those that a mesh axis runs over, the one named last changes fastest.
Arguments:
- counts: int32 [192, 48, 1024], P('orig', None, 'dest'), may hold values from 0 to 96, as said below
- anchor_factor: float32 [192, 32], P('orig'), may hold values from 0.3 to 3
- dest_factor: float32 [1024, 32], P(('dest', 'orig')), may hold values from 0.3 to 3
- hour_factor: float32 [48, 32], replicated, may hold values from 0.3 to 3
- weights: float32 [32], replicated, may hold values from 0.06 to 0.5
Outputs:
- anchor_out: float32 [192, 32], P('orig')
- dest_out: float32 [1024, 32], P(('dest', 'orig'))
- hour_out: float32 [48, 32], replicated
- weights_out: float32 [32], replicated
Inputs may be any that keep to these rules, and one draw needn't show every extreme that they name: `counts`: whole numbers of trips; many entries are zero.
All inputs are finite; a program needn't handle non-finite values.
Results may differ from a plain program's by a relative error of at most 0.00015.
Values sent between devices are 32-bit elements; how exact they have to be, the bound alone decides.
A program may use at most 64 MiB of HBM per device.

v0:
```python
import jax
import jax.numpy as jnp
from jax import lax
from jax.sharding import PartitionSpec as P

INNER = 2
OUTER = 2


HIGH = lax.Precision.HIGHEST


def ratio_of(values, left, right, full_rows):
    rows = left.shape[0] * right.shape[0]
    khatri = (left[:, None, :] * right[None, :, :]).reshape(rows, left.shape[1])
    model = lax.dot_general(khatri, full_rows, (((1,), (1,)), ((), ())), precision=HIGH)
    return (values / model, khatri)


def on_device(counts, anchor_factor, dest_factor, hour_factor, weights):
    orig_count = lax.axis_size("orig")
    dest_count = lax.axis_size("dest")
    nrow, nhour, ncol = counts.shape
    total_rows = nrow * orig_count
    total_cols = ncol * dest_count
    values = counts.astype(jnp.float32).reshape(nrow * nhour, ncol)
    anchor = anchor_factor
    hour = hour_factor
    weight = weights
    own_rows = dest_factor
    piece = own_rows.shape[0]
    dest_full = lax.all_gather(own_rows, "orig", axis=0, tiled=True)
    for outer in range(OUTER):
        growth = anchor * weight[None, :]
        for inner in range(INNER):
            ratio, khatri = ratio_of(values, growth, hour, dest_full)
            along = jnp.dot(ratio, dest_full, precision=HIGH).reshape(nrow, nhour, -1)
            partial_value = jnp.sum(along * hour[None, :, :], axis=1) / (nhour * total_cols)
            growth = growth * lax.psum(partial_value, "dest")
        total = lax.psum(jnp.sum(growth, axis=0), "orig")
        weight = total / total_rows
        anchor = growth / weight[None, :]
        growth_full = dest_full * weight[None, :]
        growth_rows = own_rows * weight[None, :]
        for inner in range(INNER):
            ratio, khatri = ratio_of(values, anchor, hour, growth_full)
            partial_value = lax.dot_general(
                ratio, khatri, (((0,), (0,)), ((), ())), precision=HIGH
            ) / (total_rows * nhour)
            growth_full = growth_full * lax.psum(partial_value, "orig")
        growth_rows = lax.dynamic_slice_in_dim(
            growth_full, lax.axis_index("orig") * piece, piece, 0
        )
        total = lax.psum(jnp.sum(growth_rows, axis=0), ("orig", "dest"))
        weight = total / total_cols
        own_rows = growth_rows / weight[None, :]
        dest_full = growth_full / weight[None, :]
        growth = hour * weight[None, :]
        for inner in range(INNER):
            ratio, khatri = ratio_of(values, anchor, growth, dest_full)
            along = jnp.dot(ratio, dest_full, precision=HIGH).reshape(nrow, nhour, -1)
            partial_value = jnp.sum(along * anchor[:, None, :], axis=0) / (total_rows * total_cols)
            growth = growth * lax.psum(partial_value, ("orig", "dest"))
        weight = jnp.sum(growth, axis=0) / nhour
        hour = growth / weight[None, :]
    return (anchor, own_rows, hour, weight)


def solution(mesh):
    return jax.shard_map(
        on_device,
        mesh=mesh,
        in_specs=(P("orig", None, "dest"), P("orig", None), P(("dest", "orig"), None), P(), P()),
        out_specs=(P("orig", None), P(("dest", "orig"), None), P(), P()),
        check_vma=False,
    )
```

profile of v0, /device:TPU:0, one launch (start us, length us, event | category | flops | bytes accessed | tf_op | source)
XLA Modules:
  0.0 482.7 jit_solution(15943761914771713764)
XLA Ops:
  0.7 1.4 convert_element_type.3
  2.1 15.7 %all_gather.3 = f32[256,32]{1,0:T(8,128)S(1)} all-gather(f32[32,32]{1,0:T(8,128)S(1)} %copy-done.1), channel_id=1, replica_groups=mesh['orig'=8,'dest'=4] {'orig'}, dimensions={0}, use_global_device_ids=true | all-gather | bytes 36864 | tf_op jit(solution)/shard_map/all_gather | solution.py:32
  19.5 1.2 fusion.16
  21.1 16.0 %psum.112 = f32[24,32]{0,1:T(8,128)S(1)} all-reduce(f32[24,32]{0,1:T(8,128)S(1)} %broadcast_multiply_fusion.20), channel_id=1, replica_groups=mesh['orig'=8,'dest'=4] {'dest'}, use_global_device_ids=true, to_apply=%region_1.0 | all-reduce | flops 768 | bytes 6144 | tf_op jit(solution)/shard_map/psum | solution.py:39
  38.7 1.2 fusion.17
  40.3 13.7 %psum.113 = f32[24,32]{0,1:T(8,128)S(1)} all-reduce(f32[24,32]{0,1:T(8,128)S(1)} %broadcast_multiply_fusion.19), channel_id=1, replica_groups=mesh['orig'=8,'dest'=4] {'dest'}, use_global_device_ids=true, to_apply=%region_3.0 | all-reduce | flops 768 | bytes 6144 | tf_op jit(solution)/shard_map/psum | solution.py:39
  54.1 13.6 %psum.114 = f32[32]{0:T(128)S(1)} all-reduce(f32[32]{0:T(128)S(1)} %get-tuple-element.18), channel_id=1, replica_groups=mesh['orig'=8,'dest'=4] {'orig'}, use_global_device_ids=true, to_apply=%region_5.0 | all-reduce | flops 32 | bytes 256 | tf_op jit(solution)/shard_map/psum | solution.py:40
  68.2 1.2 convolution_divide_fusion.9
  70.1 25.9 %psum.115 = f32[256,32]{0,1:T(8,128)S(1)} all-reduce(f32[256,32]{0,1:T(8,128)S(1)} %convolution_multiply_fusion.3), channel_id=1, replica_groups=mesh['orig'=8,'dest'=4] {'orig'}, use_global_device_ids=true, to_apply=%region_6.0 | all-reduce | flops 8192 | bytes 65536 | tf_op jit(solution)/shard_map/psum | solution.py:50
  98.0 25.9 %psum.116 = f32[256,32]{0,1:T(8,128)S(1)} all-reduce(f32[256,32]{0,1:T(8,128)S(1)} %convolution_multiply_fusion.2), channel_id=1, replica_groups=mesh['orig'=8,'dest'=4] {'orig'}, use_global_device_ids=true, to_apply=%region_7.0 | all-reduce | flops 8192 | bytes 65536 | tf_op jit(solution)/shard_map/psum | solution.py:50
  124.2 37.4 %psum.117 = f32[32]{0:T(128)S(1)} all-reduce(f32[32]{0:T(128)S(1)} %dynamic-slice_reduce_fusion), channel_id=1, replica_groups=mesh['orig'=8,'dest'=4] {'orig','dest'}, use_global_device_ids=true, to_apply=%region_9.0 | all-reduce | flops 32 | bytes 256 | tf_op jit(solution)/shard_map/psum | solution.py:54
  162.0 1.2 convolution_divide_fusion.7
  164.7 41.5 %psum.118 = f32[48,32]{0,1:T(8,128)S(1)} all-reduce(f32[48,32]{0,1:T(8,128)S(1)} %broadcast_multiply_fusion.15), channel_id=1, replica_groups=mesh['orig'=8,'dest'=4] {'orig','dest'}, use_global_device_ids=true, to_apply=%region_11.0 | all-reduce | flops 1536 | bytes 12288 | tf_op jit(solution)/shard_map/psum | solution.py:63
  209.4 39.4 %psum.119 = f32[48,32]{0,1:T(8,128)S(1)} all-reduce(f32[48,32]{0,1:T(8,128)S(1)} %broadcast_multiply_fusion.14), channel_id=1, replica_groups=mesh['orig'=8,'dest'=4] {'orig','dest'}, use_global_device_ids=true, to_apply=%region_13.0 | all-reduce | flops 1536 | bytes 12288 | tf_op jit(solution)/shard_map/psum | solution.py:63
  252.1 16.2 %psum.120 = f32[24,32]{0,1:T(8,128)S(1)} all-reduce(f32[24,32]{0,1:T(8,128)S(1)} %broadcast_multiply_fusion.18), channel_id=1, replica_groups=mesh['orig'=8,'dest'=4] {'dest'}, use_global_device_ids=true, to_apply=%region_16.0 | all-reduce | flops 768 | bytes 6144 | tf_op jit(solution)/shard_map/psum | solution.py:39
  271.5 14.1 %psum.121 = f32[24,32]{0,1:T(8,128)S(1)} all-reduce(f32[24,32]{0,1:T(8,128)S(1)} %broadcast_multiply_fusion.17), channel_id=1, replica_groups=mesh['orig'=8,'dest'=4] {'dest'}, use_global_device_ids=true, to_apply=%region_18.0 | all-reduce | flops 768 | bytes 6144 | tf_op jit(solution)/shard_map/psum | solution.py:39
  285.7 13.6 %psum.122 = f32[32]{0:T(128)S(1)} all-reduce(f32[32]{0:T(128)S(1)} %get-tuple-element.14), channel_id=1, replica_groups=mesh['orig'=8,'dest'=4] {'orig'}, use_global_device_ids=true, to_apply=%region_20.0 | all-reduce | flops 32 | bytes 256 | tf_op jit(solution)/shard_map/psum | solution.py:40
  299.7 1.2 convolution_divide_fusion.3
  301.7 25.9 %psum.123 = f32[256,32]{0,1:T(8,128)S(1)} all-reduce(f32[256,32]{0,1:T(8,128)S(1)} %convolution_multiply_fusion.1), channel_id=1, replica_groups=mesh['orig'=8,'dest'=4] {'orig'}, use_global_device_ids=true, to_apply=%region_21.0 | all-reduce | flops 8192 | bytes 65536 | tf_op jit(solution)/shard_map/psum | solution.py:50
  327.6 1.2 convolution_divide_fusion.2
  329.5 25.9 %psum.124 = f32[256,32]{0,1:T(8,128)S(1)} all-reduce(f32[256,32]{0,1:T(8,128)S(1)} %convolution_multiply_fusion), channel_id=1, replica_groups=mesh['orig'=8,'dest'=4] {'orig'}, use_global_device_ids=true, to_apply=%region_22.0 | all-reduce | flops 8192 | bytes 65536 | tf_op jit(solution)/shard_map/psum | solution.py:50
  355.8 36.8 %psum.125 = f32[32]{0:T(128)S(1)} all-reduce(f32[32]{0:T(128)S(1)} %dynamic-slice_reduce_fusion.1), channel_id=1, replica_groups=mesh['orig'=8,'dest'=4] {'orig','dest'}, use_global_device_ids=true, to_apply=%region_24.0 | all-reduce | flops 32 | bytes 256 | tf_op jit(solution)/shard_map/psum | solution.py:54
  395.8 42.5 %psum.126 = f32[48,32]{0,1:T(8,128)S(1)} all-reduce(f32[48,32]{0,1:T(8,128)S(1)} %broadcast_multiply_fusion.13), channel_id=1, replica_groups=mesh['orig'=8,'dest'=4] {'orig','dest'}, use_global_device_ids=true, to_apply=%region_26.0 | all-reduce | flops 1536 | bytes 12288 | tf_op jit(solution)/shard_map/psum | solution.py:63
  441.5 38.6 %psum.127 = f32[48,32]{0,1:T(8,128)S(1)} all-reduce(f32[48,32]{0,1:T(8,128)S(1)} %broadcast_multiply_fusion.12), channel_id=1, replica_groups=mesh['orig'=8,'dest'=4] {'orig','dest'}, use_global_device_ids=true, to_apply=%region_28.0 | all-reduce | flops 1536 | bytes 12288 | tf_op jit(solution)/shard_map/psum | solution.py:63
  (103 shorter events, 29.6 us)
Async XLA Ops:
  0.6 1.4 copy-start.1
  0.6 17.2 %copy-start.2 = (f32[24,32]{1,0:T(8,128)S(1)}, f32[24,32]{1,0:T(8,128)}, u32[]{:S(2)}) copy-start(f32[24,32]{1,0:T(8,128)} %param.6) | copy-start | bytes 9220
  0.7 17.2 %copy-start.3 = (f32[32]{0:T(128)S(1)}, f32[32]{0:T(128)}, u32[]{:S(2)}) copy-start(f32[32]{0:T(128)} %param.9) | copy-start | bytes 388
  0.7 17.3 %copy-start = (f32[48,32]{0,1:T(8,128)S(1)}, f32[48,32]{0,1:T(8,128)}, u32[]{:S(2)}) copy-start(f32[48,32]{0,1:T(8,128)} %param.8) | copy-start | bytes 18436
  480.2 2.1 copy-start.4
where the time goes:
time: 492 us; the launch traced here: 483 us
  blocking collectives  443 us (90%)
  matrix products  26.2 us (5%)
  other arithmetic  7.1 us (1%)
    psum x4, blocking collectives, on_device(): growth = growth * lax.psum(partial_value, ('orig', 'dest'))  162 us
    psum x4, blocking collectives, on_device(): growth_full = growth_full * lax.psum(partial_value, 'orig')  104 us
    psum x2, blocking collectives, on_device(): total = lax.psum(jnp.sum(growth_rows, axis=0), ('orig', 'dest'))  74.2 us
    psum x4, blocking collectives, on_device(): growth = growth * lax.psum(partial_value, 'dest')  60.1 us
    psum x2, blocking collectives, on_device(): total = lax.psum(jnp.sum(growth, axis=0), 'orig')  27.2 us
    all_gather x1, blocking collectives, on_device(): dest_full = lax.all_gather(own_rows, 'orig', axis=0, tiled=True)  15.7 us
    dot_general x12, matrix products, ratio_of(): lax.dot_general(khatri, full_rows, (((1,), (1,)), ((), ())), precision=HIGH)  14 us

commit v1 on v0

v1 whole, which is shorter than its diff:
```python
import functools

import jax
import jax.numpy as jnp
from jax import lax
from jax.experimental import pallas as pl
from jax.experimental.pallas import tpu as pltpu
from jax.sharding import PartitionSpec as P

INNER = 2
OUTER = 2
LANES = 128
F32 = jnp.float32
BF16 = jnp.bfloat16
HIGH = lax.Precision.HIGHEST
MESH = pl.DeviceIdType.MESH


def iota(shape, dim):
    return lax.broadcasted_iota(jnp.int32, shape, dim)


def kernel(nz, ndest, counts_ref, anchor_ref, dest_ref, hour_ref, weight_ref,
           anchor_out, dest_out, hour_out, weight_out,
           vals, outbox, ucur, ccur, tcur, bmod, balo, phis, acc, hacc,
           xbuf, zbuf, hbuf, abuf,
           x_send, x_recv, z_send, z_recv, h_send, h_recv, v_send, v_recv, a_sem):
    nrow, nhour, ncol = counts_ref.shape
    rank = hour_ref.shape[1]
    piece = dest_ref.shape[0]
    copies = LANES // rank
    half = ncol // 2
    nx = 2 * ndest
    total_rows = nrow * 2 * nz
    total_cols = ncol * ndest
    me_orig = lax.axis_index("orig")
    me_dest = lax.axis_index("dest")
    zi = me_orig // 2
    core = me_orig % 2
    xi = me_dest * 2 + core
    partner = {"orig": zi * 2 + (1 - core)}
    chunks = vals.shape[1] // (8 * nhour)
    crow = 8 * nhour

    def xpeer(t):
        idx = (xi + t) % nx
        return idx, {"orig": zi * 2 + idx % 2, "dest": idx // 2}

    def zpeer(t):
        idx = (zi + t) % nz
        return idx, {"orig": idx * 2 + core}

    barrier = pltpu.get_barrier_semaphore()
    for t in range(1, nx):
        pl.semaphore_signal(barrier, inc=1, device_id=xpeer(t)[1], device_id_type=MESH)
    for t in range(1, nz):
        pl.semaphore_signal(barrier, inc=1, device_id=zpeer(t)[1], device_id_type=MESH)

    def copy(ref, mine, theirs, send, recv, t, who):
        return pltpu.make_async_remote_copy(
            src_ref=ref.at[mine], dst_ref=ref.at[mine] if theirs is None else ref.at[theirs],
            send_sem=send.at[t - 1], recv_sem=recv.at[mine if theirs is None else theirs],
            device_id=who, device_id_type=MESH)

    def start(ref, send, recv, peer, n, me):
        for t in range(1, n):
            copy(ref, me, None, send, recv, t, peer(t)[1]).start()

    def collect(ref, send, recv, peer, n, me):
        for t in range(1, n):
            idx, who = peer(t)
            copy(ref, idx, None, send, recv, t, who).wait_recv()
        total = ref[0]
        for s in range(1, n):
            total = total + ref[s]
        return total

    def finish(ref, send, recv, peer, n, me):
        for t in range(1, n):
            copy(ref, me, None, send, recv, t, peer(t)[1]).wait_send()

    lane = iota((1, LANES), 1)
    group = lane // rank
    spread = (iota((rank, LANES), 1) % rank == iota((rank, LANES), 0)).astype(F32)
    diag = iota((rank, LANES), 1) == iota((rank, LANES), 0)
    diag_all = iota((rank, LANES), 1) % rank == iota((rank, LANES), 0)

    def to_column(row):
        return jnp.sum(jnp.where(diag, jnp.broadcast_to(row, (rank, LANES)), 0.0), axis=1, keepdims=True)

    def to_row(column):
        return jnp.sum(jnp.where(diag_all, jnp.broadcast_to(column, (rank, LANES)), 0.0), axis=0, keepdims=True)

    def spread_group(x, b):
        x = jnp.where(group == b, x, 0.0)
        step = rank
        while step < LANES:
            x = x + pltpu.roll(x, step, 1)
            step *= 2
        return x

    def pair_up(x):
        return x + pltpu.roll(x, rank, 1)

    def twice(x):
        return jnp.concatenate([x, x], axis=1)

    hrow = -(-nhour // (8 * (copies - 1))) * 8
    hblocks = nhour // hrow
    ablocks = nrow // 8

    def pack_hour(p, extra):
        out = jnp.broadcast_to(extra, (hrow, LANES))
        for b in range(hblocks):
            out = jnp.where(group == b, p[b * hrow:(b + 1) * hrow], out)
        return out

    def unpack_hour(s):
        return jnp.concatenate([spread_group(s, b) for b in range(hblocks)], axis=0)

    def pack_anchor(p):
        sides = []
        for g in range(2):
            side = p[:8, g * LANES:(g + 1) * LANES]
            for b in range(1, ablocks):
                side = jnp.where(group == b, p[8 * b:8 * b + 8, g * LANES:(g + 1) * LANES], side)
            sides.append(side)
        return jnp.concatenate(sides, axis=0)

    def unpack_anchor(s):
        sides = []
        for g in range(2):
            part = s[8 * g:8 * g + 8]
            sides.append(jnp.concatenate([spread_group(part, b) for b in range(ablocks)], axis=0))
        return jnp.concatenate(sides, axis=1)

    own_anchor = lax.dot(anchor_ref[...], spread, precision=HIGH)
    weight_row = jnp.sum(jnp.where(
        diag_all, jnp.broadcast_to(to_rows(weight_ref[...], rank), (rank, LANES)), 0.0), axis=0, keepdims=True)
    abuf[core] = own_anchor * weight_row
    ccur[...] = twice(lax.dot(hour_ref[...], spread, precision=HIGH))
    place = (iota((piece, LANES), 1) == zi * piece + iota((piece, LANES), 0)).astype(F32)
    zbuf[0, zi] = jnp.concatenate([
        lax.dot_general(dest_ref[...], place, (((0,), (0,)), ((), ())), precision=HIGH),
        jnp.zeros((8, LANES), F32)], axis=0)

    dst = iota((ncol, ncol), 1)
    src = iota((ncol, ncol), 0)
    local = dst % half
    side = dst // half
    parity = (core + side) % 2
    wanted = local + (local // piece + parity) * piece
    perm = (src == wanted).astype(F32).astype(BF16)

    pl.semaphore_wait(barrier, nx - 1 + nz - 1)

    start(zbuf.at[0], z_send.at[0], z_recv.at[0], zpeer, nz, zi)

    def acopy(slot):
        return pltpu.make_async_remote_copy(
            src_ref=abuf.at[slot], dst_ref=abuf.at[slot], send_sem=a_sem.at[0], recv_sem=a_sem.at[1],
            device_id=partner, device_id_type=MESH)

    acopy(core).start()

    def vcopy(s, slot):
        return pltpu.make_async_remote_copy(
            src_ref=outbox.at[pl.ds(s * crow, crow)],
            dst_ref=vals.at[slot, pl.ds(s * crow, crow)],
            send_sem=v_send.at[s], recv_sem=v_recv.at[s],
            device_id=partner, device_id_type=MESH)

    for s in range(chunks):
        block = counts_ref[8 * s:8 * s + 8].reshape(crow, ncol).astype(F32).astype(BF16)
        moved = jnp.dot(block, perm, preferred_element_type=F32)
        outbox[s * crow:(s + 1) * crow] = moved[:, half:]
        vals[core, s * crow:(s + 1) * crow] = moved[:, :half]
        vcopy(s, core).start()

    zero = jnp.zeros((LANES, LANES), BF16)
    for ref in (bmod, balo):
        ref[:LANES, LANES:] = zero
        ref[LANES:, :LANES] = zero

    def set_right(t):
        hi = t.astype(BF16).astype(F32)
        lo = t - hi
        model = jnp.concatenate([hi] * (copies // 2) + [lo] * (copies // 2), axis=0).astype(BF16)
        along = jnp.concatenate([hi, lo] * (copies // 2), axis=0).astype(BF16)
        for ref, x in ((bmod, model), (balo, along)):
            ref[:LANES, :LANES] = x
            ref[LANES:, LANES:] = x

    high_lane = (iota((1, 2 * LANES), 1) // rank) % 2 == 0

    def ratio_chunk(s):
        i0 = pl.multiple_of(s * 8, 8)
        r0 = pl.multiple_of(s * crow, crow)
        left = ucur[pl.ds(i0, 8), :]
        kh = (left[:, None, :] * ccur[...][None, :, :]).reshape(crow, 2 * LANES)
        hi = kh.astype(BF16).astype(F32)
        khs = jnp.where(high_lane, hi, kh - hi).astype(BF16)
        model = jnp.dot(khs, bmod[...], preferred_element_type=F32)
        values = jnp.concatenate([vals[0, pl.ds(r0, crow), :], vals[1, pl.ds(r0, crow), :]], axis=1)
        ratio = values / model
        rh = ratio.astype(BF16)
        rl = (ratio - rh.astype(F32)).astype(BF16)
        return i0, left, khs, rh, rl

    def along_of(rh, rl):
        dims = (((1,), (1,)), ((), ()))
        return (lax.dot_general(rh, balo[...], dims, preferred_element_type=F32)
                + lax.dot_general(rl, balo[...], dims, preferred_element_type=F32))

    def anchor_phi():
        @pl.loop(0, chunks)
        def _(s):
            i0, left, khs, rh, rl = ratio_chunk(s)
            along = along_of(rh, rl).reshape(8, nhour, 2 * LANES)
            phis[pl.ds(i0, 8), :] = jnp.sum(along * ccur[...][None, :, :], axis=1)
        p = phis[...]
        return jnp.concatenate([pair_up(p[:, :LANES]), pair_up(p[:, LANES:])], axis=1)

    def hour_phi():
        hacc[...] = jnp.zeros_like(hacc)

        @pl.loop(0, chunks)
        def _(s):
            i0, left, khs, rh, rl = ratio_chunk(s)
            along = along_of(rh, rl).reshape(8, nhour, 2 * LANES)
            hacc[...] += jnp.sum(along * left[:, None, :], axis=0)
        p = hacc[...]
        return pair_up(p[:, :LANES] + p[:, LANES:])

    def dest_phi():
        acc[...] = jnp.zeros_like(acc)
        dims = (((0,), (0,)), ((), ()))

        @pl.loop(0, chunks)
        def _(s):
            i0, left, khs, rh, rl = ratio_chunk(s)
            total = acc[...]
            for g in range(2):
                lanes = slice(g * LANES, (g + 1) * LANES)
                total = total + lax.dot_general(khs[:, lanes], rh[:, lanes], dims, preferred_element_type=F32)
                total = total + lax.dot_general(khs[:, lanes], rl[:, lanes], dims, preferred_element_type=F32)
            acc[...] = total
        return acc[:rank] + acc[rank:2 * rank]

    acopy(1 - core).wait_recv()
    ucur[...] = jnp.concatenate([abuf[0], abuf[1]], axis=1)
    gathered = collect(zbuf.at[0], z_send.at[0], z_recv.at[0], zpeer, nz, zi)
    tcur[...] = gathered[:rank]
    set_right(tcur[...])
    for s in range(chunks):
        vcopy(s, 1 - core).wait_recv()

    @pl.loop(0, OUTER)
    def _(outer):
        for inner in range(INNER):
            e = outer * 4 + inner
            xb, xs, xr = xbuf.at[e], x_send.at[e], x_recv.at[e]
            xb[xi] = pack_anchor(anchor_phi())
            start(xb, xs, xr, xpeer, nx, xi)
            s = collect(xb, xs, xr, xpeer, nx, xi)
            ucur[...] = ucur[...] * (unpack_anchor(s) / (nhour * total_cols))
        col = jnp.sum(ucur[...], axis=0, keepdims=True)
        col = col[:, :LANES] + col[:, LANES:]
        anchor_w = None
        for inner in range(INNER):
            e = 1 + outer * 2 + inner
            zb, zs, zr = zbuf.at[e], z_send.at[e], z_recv.at[e]
            zb[zi] = jnp.concatenate([dest_phi(), jnp.broadcast_to(col, (8, LANES))], axis=0)
            start(zb, zs, zr, zpeer, nz, zi)
            s = collect(zb, zs, zr, zpeer, nz, zi)
            growth = tcur[...] * (s[:rank] / (total_rows * nhour))
            if inner == 0:
                anchor_w = s[rank:rank + 1] / total_rows
                growth = growth / to_column(anchor_w)
            tcur[...] = growth
            set_right(growth)
        ucur[...] = ucur[...] / twice(anchor_w)
        dest_col = to_row(jnp.sum(tcur[...], axis=1, keepdims=True))
        dest_w = None
        for inner in range(INNER):
            e = outer * 4 + 2 + inner
            xb, xs, xr = xbuf.at[e], x_send.at[e], x_recv.at[e]
            xb[xi] = pack_hour(hour_phi(), dest_col)
            start(xb, xs, xr, xpeer, nx, xi)
            s = collect(xb, xs, xr, xpeer, nx, xi)
            h = outer * 2 + inner
            hb, hs, hr = hbuf.at[h], h_send.at[h], h_recv.at[h]
            hb[zi] = s
            start(hb, hs, hr, zpeer, nz, zi)
            if inner == 0:
                dest_w = spread_group(s[:1], copies - 1) / total_cols
            s = collect(hb, hs, hr, zpeer, nz, zi)
            growth = ccur[:, :LANES] * (unpack_hour(s) / (total_rows * total_cols))
            if inner == 0:
                growth = growth / dest_w
            ccur[...] = twice(growth)
        w = jnp.sum(ccur[:, :LANES], axis=0, keepdims=True) / nhour
        ccur[...] = ccur[...] / twice(w)
        tcur[...] = tcur[...] / to_column(dest_w)
        weight_out[...] = w[:, :rank]

        @pl.when(outer == OUTER - 1)
        def _():
            mine = jnp.where(core == 0, ucur[:, :LANES], ucur[:, LANES:])
            anchor_out[...] = mine[:, :rank]
            hour_out[...] = ccur[:, :rank]
            dest_out[...] = lax.dot_general(
                place, tcur[...], (((1,), (1,)), ((), ())), precision=HIGH)

        @pl.when(outer < OUTER - 1)
        def _():
            ucur[...] = ucur[...] * twice(w)
            set_right(tcur[...])

    acopy(core).wait_send()
    for s in range(chunks):
        vcopy(s, core).wait_send()
    finish(zbuf.at[0], z_send.at[0], z_recv.at[0], zpeer, nz, zi)

    @pl.loop(0, OUTER * 4)
    def _(e):
        finish(xbuf.at[e], x_send.at[e], x_recv.at[e], xpeer, nx, xi)

    @pl.loop(0, OUTER * 2)
    def _(e):
        finish(zbuf.at[1 + e], z_send.at[1 + e], z_recv.at[1 + e], zpeer, nz, zi)
        finish(hbuf.at[e], h_send.at[e], h_recv.at[e], zpeer, nz, zi)


def to_rows(row, rank):
    square = jnp.where(iota((rank, rank), 0) == iota((rank, rank), 1), jnp.broadcast_to(row, (rank, rank)), 0.0)
    return jnp.sum(square, axis=1, keepdims=True)


def on_device(counts, anchor_factor, dest_factor, hour_factor, weights):
    norig = lax.axis_size("orig")
    ndest = lax.axis_size("dest")
    nz, nx = norig // 2, 2 * ndest
    nrow, nhour, ncol = counts.shape
    rank = hour_factor.shape[1]
    rows = nrow * nhour
    chunks = nrow // 8
    hrow = -(-nhour // (8 * (LANES // rank - 1))) * 8
    dma = pltpu.SemaphoreType.DMA
    vmem = pltpu.VMEM
    outs = pl.pallas_call(
        functools.partial(kernel, nz, ndest),
        out_shape=[
            jax.ShapeDtypeStruct(anchor_factor.shape, F32),
            jax.ShapeDtypeStruct(dest_factor.shape, F32),
            jax.ShapeDtypeStruct(hour_factor.shape, F32),
            jax.ShapeDtypeStruct((1, rank), F32),
        ],
        in_specs=[pl.BlockSpec(memory_space=pltpu.VMEM)] * 5,
        out_specs=[pl.BlockSpec(memory_space=pltpu.VMEM)] * 4,
        scratch_shapes=[
            vmem((2, rows, LANES), F32),
            vmem((rows, LANES), F32),
            vmem((nrow, 2 * LANES), F32),
            vmem((nhour, 2 * LANES), F32),
            vmem((rank, LANES), F32),
            vmem((2 * LANES, 2 * LANES), BF16),
            vmem((2 * LANES, 2 * LANES), BF16),
            vmem((nrow, 2 * LANES), F32),
            vmem((LANES, LANES), F32),
            vmem((nhour, 2 * LANES), F32),
            vmem((OUTER * 4, nx, hrow, LANES), F32),
            vmem((1 + OUTER * 2, nz, rank + 8, LANES), F32),
            vmem((OUTER * 2, nz, hrow, LANES), F32),
            vmem((2, nrow, LANES), F32),
            dma((OUTER * 4, nx - 1)), dma((OUTER * 4, nx)),
            dma((1 + OUTER * 2, nz - 1)), dma((1 + OUTER * 2, nz)),
            dma((OUTER * 2, nz - 1)), dma((OUTER * 2, nz)),
            dma((chunks,)), dma((chunks,)), dma((2,)),
        ],
        compiler_params=pltpu.CompilerParams(
            collective_id=0, has_side_effects=True, vmem_limit_bytes=48 * 1024 * 1024),
    )(counts, anchor_factor, dest_factor, hour_factor, weights.reshape(1, rank))
    return outs[0], outs[1], outs[2], outs[3].reshape(rank)


def solution(mesh):
    return jax.shard_map(
        on_device,
        mesh=mesh,
        in_specs=(P("orig", None, "dest"), P("orig", None), P(("dest", "orig"), None), P(), P()),
        out_specs=(P("orig", None), P(("dest", "orig"), None), P(), P()),
        check_vma=False,
    )
```

time: 492 us -> 93.8 us (0.19); the launches traced: 483 us -> 93.4 us
  blocking collectives: 443 us -> 0 us
  Pallas kernels: 0 us -> 86.2 us
  matrix products: 26.2 us -> 0 us
  other arithmetic: 7.1 us -> 0 us
    psum x16 -> x0, blocking collectives: 427 us -> none  [the longest x4 162 us: on_device(): growth = growth * lax.psum(partial_value, ('orig', 'dest'))]
    pallas_call x0 -> x1, Pallas kernels: none -> 86.2 us  [on_device(): pl.pallas_call(functools.partial(kernel, nz, ndest), out_shape=[jax.Shape...]
    dot_general x24 -> x0, matrix products: 26.2 us -> none  [the longest x12 14 us: ratio_of(): lax.dot_general(khatri, full_rows, (((1,), (1,)), ((), ())), precision=HIGH)]
    all_gather x1 -> x0, blocking collectives: 15.7 us -> none  [on_device(): dest_full = lax.all_gather(own_rows, 'orig', axis=0, tiled=True)]
    unnamed x13, local copies, waits for them, and re-layouts: 1.45 us -> 6.54 us
where the time goes in v1:
time: 93.8 us; the launch traced here: 93.4 us
  Pallas kernels  86.2 us (92%)
  local copies, waits for them, and re-layouts  6.54 us (7%)
    pallas_call x1, Pallas kernels, on_device(): pl.pallas_call(functools.partial(kernel, nz, ndest), out_shape=[jax.Shape...  86.2 us
    unnamed x13, local copies, waits for them, and re-layouts  6.54 us

profile of v1, /device:TPU:0, one launch (start us, length us, event | category | flops | bytes accessed | tf_op | source)
XLA Modules:
  0.0 93.4 jit_solution(14284087949383930922)
XLA Ops:
  0.6 0.8 copy.9.hour_ref
  1.4 0.0 copy-start
  1.4 1.3 %copy-done = s32[24,48,256]{2,1,0:T(8,128)S(1)} copy-done((s32[24,48,256]{2,1,0:T(8,128)S(1)}, s32[24,48,256]{2,1,0:T(8,128)}, u32[]{:S(2)}) %copy-start) | copy-done | bytes 1179672
  2.7 0.0 copy-start.1
  2.7 0.7 copy-done.1
  3.4 0.0 copy-start.2
  3.4 0.7 copy-done.2
  4.1 0.0 copy-start.3
  4.1 0.7 copy-done.3
  4.8 86.2 %shard_map.84 = (f32[24,32]{1,0:T(8,128)S(1)}, f32[32,32]{1,0:T(8,128)S(1)}, f32[48,32]{1,0:T(8,128)S(1)}, f32[1,32]{1,0:T(1,128)S(1)}) custom-call(s32[24,48,256]{2,1,0:T(8,128)S(1)} %copy-done, f32[24,32]{1,0:T(8,128)S(1)} %copy-done.2, f32[32,32]{1,0:T(8,128)S(1)} %copy-done.1, f32[48,32]{1,0:T(8,128)S(1)} %copy.9.hour_ref, f32[1,32]{1,0:T(1,128)S(1)} %bitcast.2), custom_call_target="tpu_custom_call" | custom-call | tf_op jit(solution)/shard_map/pallas_call | solution.py:351
  91.0 0.7 copy.10
  91.7 0.6 copy.14
  92.3 0.6 copy.15
  92.9 0.5 copy.16
Async XLA Ops:
  1.4 1.3 %copy-start = (s32[24,48,256]{2,1,0:T(8,128)S(1)}, s32[24,48,256]{2,1,0:T(8,128)}, u32[]{:S(2)}) copy-start(s32[24,48,256]{2,1,0:T(8,128)} %counts_ref.1) | copy-start | bytes 3538948
  2.7 0.7 copy-start.1
  3.4 0.7 copy-start.2
  4.1 0.7 copy-start.3

commit v2 on v1

--- a/solution.py
+++ b/solution.py
@@ -20,13 +20,13 @@
     return lax.broadcasted_iota(jnp.int32, shape, dim)
 
 
-def kernel(nz, ndest, counts_ref, anchor_ref, dest_ref, hour_ref, weight_ref,
+def kernel(nz, ndest, counts_in, anchor_in, dest_in, hour_in, weight_in,
            anchor_out, dest_out, hour_out, weight_out,
-           vals, outbox, ucur, ccur, tcur, bmod, balo, phis, acc, hacc,
-           xbuf, zbuf, hbuf, abuf,
-           x_send, x_recv, z_send, z_recv, h_send, h_recv, v_send, v_recv, a_sem):
+           vals, outbox, ucur, ccur, tcur, bmod, balo,
+           xbuf, zbuf, hbuf, abuf, counts_ref, anchor_ref, dest_ref, hour_ref, weight_ref,
+           x_send, x_recv, z_send, z_recv, h_send, h_recv, v_send, v_recv, a_sem, in_sem):
     nrow, nhour, ncol = counts_ref.shape
-    rank = hour_ref.shape[1]
+    rank = hour_ref.shape[0]
     piece = dest_ref.shape[0]
     copies = LANES // rank
     half = ncol // 2
@@ -50,6 +50,12 @@
         idx = (zi + t) % nz
         return idx, {"orig": idx * 2 + core}
 
+    small = [pltpu.make_async_copy(a, b, in_sem.at[q]) for q, (a, b) in enumerate(
+        ((anchor_in, anchor_ref), (dest_in, dest_ref), (hour_in, hour_ref), (weight_in, weight_ref)))]
+    large = [pltpu.make_async_copy(counts_in.at[pl.ds(8 * s, 8)], counts_ref.at[pl.ds(8 * s, 8)], in_sem.at[4 + s])
+             for s in range(chunks)]
+    for dma in small + large:
+        dma.start()
     barrier = pltpu.get_barrier_semaphore()
     for t in range(1, nx):
         pl.semaphore_signal(barrier, inc=1, device_id=xpeer(t)[1], device_id_type=MESH)
@@ -134,16 +140,6 @@
             sides.append(jnp.concatenate([spread_group(part, b) for b in range(ablocks)], axis=0))
         return jnp.concatenate(sides, axis=1)
 
-    own_anchor = lax.dot(anchor_ref[...], spread, precision=HIGH)
-    weight_row = jnp.sum(jnp.where(
-        diag_all, jnp.broadcast_to(to_rows(weight_ref[...], rank), (rank, LANES)), 0.0), axis=0, keepdims=True)
-    abuf[core] = own_anchor * weight_row
-    ccur[...] = twice(lax.dot(hour_ref[...], spread, precision=HIGH))
-    place = (iota((piece, LANES), 1) == zi * piece + iota((piece, LANES), 0)).astype(F32)
-    zbuf[0, zi] = jnp.concatenate([
-        lax.dot_general(dest_ref[...], place, (((0,), (0,)), ((), ())), precision=HIGH),
-        jnp.zeros((8, LANES), F32)], axis=0)
-
     dst = iota((ncol, ncol), 1)
     src = iota((ncol, ncol), 0)
     local = dst % half
@@ -152,6 +148,25 @@
     wanted = local + (local // piece + parity) * piece
     perm = (src == wanted).astype(F32).astype(BF16)
 
+    def arrange(s):
+        large[s].wait()
+        block = counts_ref[8 * s:8 * s + 8].reshape(crow, ncol).astype(F32).astype(BF16)
+        moved = jnp.dot(block, perm, preferred_element_type=F32)
+        outbox[s * crow:(s + 1) * crow] = moved[:, half:]
+        vals[core, s * crow:(s + 1) * crow] = moved[:, :half]
+
+    for dma in small:
+        dma.wait()
+    own_anchor = lax.dot(anchor_ref[...], spread, precision=HIGH)
+    weight_row = jnp.sum(jnp.where(
+        diag_all, jnp.broadcast_to(to_rows(weight_ref[...], rank), (rank, LANES)), 0.0), axis=0, keepdims=True)
+    abuf[core] = own_anchor * weight_row
+    ccur[...] = twice(lax.dot_general(hour_ref[...], spread, (((0,), (0,)), ((), ())), precision=HIGH))
+    place = (iota((piece, LANES), 1) == zi * piece + iota((piece, LANES), 0)).astype(F32)
+    zbuf[0, zi] = jnp.concatenate([
+        lax.dot_general(dest_ref[...], place, (((0,), (0,)), ((), ())), precision=HIGH),
+        jnp.zeros((8, LANES), F32)], axis=0)
+
     pl.semaphore_wait(barrier, nx - 1 + nz - 1)
 
     start(zbuf.at[0], z_send.at[0], z_recv.at[0], zpeer, nz, zi)
@@ -171,81 +186,70 @@
             device_id=partner, device_id_type=MESH)
 
     for s in range(chunks):
-        block = counts_ref[8 * s:8 * s + 8].reshape(crow, ncol).astype(F32).astype(BF16)
-        moved = jnp.dot(block, perm, preferred_element_type=F32)
-        outbox[s * crow:(s + 1) * crow] = moved[:, half:]
-        vals[core, s * crow:(s + 1) * crow] = moved[:, :half]
+        arrange(s)
         vcopy(s, core).start()
 
-    zero = jnp.zeros((LANES, LANES), BF16)
-    for ref in (bmod, balo):
-        ref[:LANES, LANES:] = zero
-        ref[LANES:, :LANES] = zero
+    bmod[...] = jnp.zeros_like(bmod)
+    balo[...] = jnp.zeros_like(balo)
 
     def set_right(t):
         hi = t.astype(BF16).astype(F32)
         lo = t - hi
         model = jnp.concatenate([hi] * (copies // 2) + [lo] * (copies // 2), axis=0).astype(BF16)
-        along = jnp.concatenate([hi, lo] * (copies // 2), axis=0).astype(BF16)
-        for ref, x in ((bmod, model), (balo, along)):
-            ref[:LANES, :LANES] = x
-            ref[LANES:, LANES:] = x
+        along = jnp.concatenate([hi, lo], axis=0).astype(BF16)
+        for g in range(2):
+            lanes = slice(g * LANES, (g + 1) * LANES)
+            bmod[lanes, lanes] = model
+            for part in range(2):
+                balo[g * 2 * rank:(g + 1) * 2 * rank, (2 * part + g) * LANES:(2 * part + g + 1) * LANES] = along
 
     high_lane = (iota((1, 2 * LANES), 1) // rank) % 2 == 0
 
     def ratio_chunk(s):
-        i0 = pl.multiple_of(s * 8, 8)
-        r0 = pl.multiple_of(s * crow, crow)
-        left = ucur[pl.ds(i0, 8), :]
+        left = ucur[8 * s:8 * s + 8]
         kh = (left[:, None, :] * ccur[...][None, :, :]).reshape(crow, 2 * LANES)
         hi = kh.astype(BF16).astype(F32)
         khs = jnp.where(high_lane, hi, kh - hi).astype(BF16)
         model = jnp.dot(khs, bmod[...], preferred_element_type=F32)
-        values = jnp.concatenate([vals[0, pl.ds(r0, crow), :], vals[1, pl.ds(r0, crow), :]], axis=1)
+        rows = slice(s * crow, (s + 1) * crow)
+        values = jnp.concatenate([vals[0, rows], vals[1, rows]], axis=1)
         ratio = values / model
         rh = ratio.astype(BF16)
         rl = (ratio - rh.astype(F32)).astype(BF16)
-        return i0, left, khs, rh, rl
+        return left, khs, rh, rl
 
     def along_of(rh, rl):
-        dims = (((1,), (1,)), ((), ()))
-        return (lax.dot_general(rh, balo[...], dims, preferred_element_type=F32)
-                + lax.dot_general(rl, balo[...], dims, preferred_element_type=F32))
+        return lax.dot_general(jnp.concatenate([rh, rl], axis=1), balo[...], (((1,), (1,)), ((), ())),
+                               preferred_element_type=F32).reshape(8, nhour, LANES)
 
     def anchor_phi():
-        @pl.loop(0, chunks)
-        def _(s):
-            i0, left, khs, rh, rl = ratio_chunk(s)
-            along = along_of(rh, rl).reshape(8, nhour, 2 * LANES)
-            phis[pl.ds(i0, 8), :] = jnp.sum(along * ccur[...][None, :, :], axis=1)
-        p = phis[...]
-        return jnp.concatenate([pair_up(p[:, :LANES]), pair_up(p[:, LANES:])], axis=1)
+        parts = []
+        for s in range(chunks):
+            left, khs, rh, rl = ratio_chunk(s)
+            parts.append(jnp.sum(along_of(rh, rl) * ccur[:, :LANES][None, :, :], axis=1))
+        p = pair_up(jnp.concatenate(parts, axis=0))
+        return jnp.concatenate([spread_group(p, 1), spread_group(p, 3)], axis=1)
 
     def hour_phi():
-        hacc[...] = jnp.zeros_like(hacc)
-
-        @pl.loop(0, chunks)
-        def _(s):
-            i0, left, khs, rh, rl = ratio_chunk(s)
-            along = along_of(rh, rl).reshape(8, nhour, 2 * LANES)
-            hacc[...] += jnp.sum(along * left[:, None, :], axis=0)
-        p = hacc[...]
-        return pair_up(p[:, :LANES] + p[:, LANES:])
+        p = None
+        for s in range(chunks):
+            left, khs, rh, rl = ratio_chunk(s)
+            mixed = jnp.where(group < 2, left[:, :LANES], left[:, LANES:])
+            part = jnp.sum(along_of(rh, rl) * mixed[:, None, :], axis=0)
+            p = part if p is None else p + part
+        return pair_up(p + pltpu.roll(p, 2 * rank, 1))
 
     def dest_phi():
-        acc[...] = jnp.zeros_like(acc)
         dims = (((0,), (0,)), ((), ()))
-
-        @pl.loop(0, chunks)
-        def _(s):
-            i0, left, khs, rh, rl = ratio_chunk(s)
-            total = acc[...]
+        total = None
+        for s in range(chunks):
+            left, khs, rh, rl = ratio_chunk(s)
             for g in range(2):
                 lanes = slice(g * LANES, (g + 1) * LANES)
-                total = total + lax.dot_general(khs[:, lanes], rh[:, lanes], dims, preferred_element_type=F32)
-                total = total + lax.dot_general(khs[:, lanes], rl[:, lanes], dims, preferred_element_type=F32)
-            acc[...] = total
-        return acc[:rank] + acc[rank:2 * rank]
+                for r in (rh, rl):
+                    part = lax.dot_general(khs[:, lanes], r[:, lanes], dims, preferred_element_type=F32)
+                    total = part if total is None else total + part
+        return total[:rank] + total[rank:2 * rank]
 
     acopy(1 - core).wait_recv()
     ucur[...] = jnp.concatenate([abuf[0], abuf[1]], axis=1)
@@ -308,7 +312,8 @@
         def _():
             mine = jnp.where(core == 0, ucur[:, :LANES], ucur[:, LANES:])
             anchor_out[...] = mine[:, :rank]
-            hour_out[...] = ccur[:, :rank]
+            hour_out[...] = lax.dot_general(
+                diag.astype(F32), ccur[:, :LANES], (((1,), (1,)), ((), ())), precision=HIGH)
             dest_out[...] = lax.dot_general(
                 place, tcur[...], (((1,), (1,)), ((), ())), precision=HIGH)
 
@@ -330,6 +335,14 @@
     def _(e):
         finish(zbuf.at[1 + e], z_send.at[1 + e], z_recv.at[1 + e], zpeer, nz, zi)
         finish(hbuf.at[e], h_send.at[e], h_recv.at[e], zpeer, nz, zi)
+
+
+def put_out(*refs):
+    copies = [pltpu.make_async_copy(refs[q], refs[4 + q], refs[8].at[q]) for q in range(4)]
+    for c in copies:
+        c.start()
+    for c in copies:
+        c.wait()
 
 
 def to_rows(row, rank):
@@ -353,10 +366,10 @@
         out_shape=[
             jax.ShapeDtypeStruct(anchor_factor.shape, F32),
             jax.ShapeDtypeStruct(dest_factor.shape, F32),
-            jax.ShapeDtypeStruct(hour_factor.shape, F32),
+            jax.ShapeDtypeStruct((rank, nhour), F32),
             jax.ShapeDtypeStruct((1, rank), F32),
         ],
-        in_specs=[pl.BlockSpec(memory_space=pltpu.VMEM)] * 5,
+        in_specs=[pl.BlockSpec(memory_space=pltpu.HBM)] * 5,
         out_specs=[pl.BlockSpec(memory_space=pltpu.VMEM)] * 4,
         scratch_shapes=[
             vmem((2, rows, LANES), F32),
@@ -365,23 +378,32 @@
             vmem((nhour, 2 * LANES), F32),
             vmem((rank, LANES), F32),
             vmem((2 * LANES, 2 * LANES), BF16),
-            vmem((2 * LANES, 2 * LANES), BF16),
-            vmem((nrow, 2 * LANES), F32),
-            vmem((LANES, LANES), F32),
-            vmem((nhour, 2 * LANES), F32),
+            vmem((4 * rank, 4 * LANES), BF16),
             vmem((OUTER * 4, nx, hrow, LANES), F32),
             vmem((1 + OUTER * 2, nz, rank + 8, LANES), F32),
             vmem((OUTER * 2, nz, hrow, LANES), F32),
             vmem((2, nrow, LANES), F32),
+            vmem(counts.shape, counts.dtype),
+            vmem(anchor_factor.shape, F32),
+            vmem(dest_factor.shape, F32),
+            vmem((rank, nhour), F32),
+            vmem((1, rank), F32),
             dma((OUTER * 4, nx - 1)), dma((OUTER * 4, nx)),
             dma((1 + OUTER * 2, nz - 1)), dma((1 + OUTER * 2, nz)),
             dma((OUTER * 2, nz - 1)), dma((OUTER * 2, nz)),
-            dma((chunks,)), dma((chunks,)), dma((2,)),
+            dma((chunks,)), dma((chunks,)), dma((2,)), dma((4 + chunks,)),
         ],
         compiler_params=pltpu.CompilerParams(
-            collective_id=0, has_side_effects=True, vmem_limit_bytes=48 * 1024 * 1024),
-    )(counts, anchor_factor, dest_factor, hour_factor, weights.reshape(1, rank))
-    return outs[0], outs[1], outs[2], outs[3].reshape(rank)
+            collective_id=0, has_side_effects=True, vmem_limit_bytes=67043328),
+    )(counts, anchor_factor, dest_factor, hour_factor.T, weights.reshape(1, rank))
+    outs = pl.pallas_call(
+        put_out,
+        out_shape=[jax.ShapeDtypeStruct(o.shape, F32) for o in outs],
+        in_specs=[pl.BlockSpec(memory_space=pltpu.VMEM)] * 4,
+        out_specs=[pl.BlockSpec(memory_space=pltpu.HBM)] * 4,
+        scratch_shapes=[dma((4,))],
+    )(*outs)
+    return outs[0], outs[1], outs[2].T, outs[3].reshape(rank)
 
 
 def solution(mesh):

time: 93.8 us -> 83.7 us (0.89)
  local copies, waits for them, and re-layouts: 6.54 us -> 0 us
  Pallas kernels: 86.2 us -> 82.8 us
    unnamed x13 -> x0, local copies, waits for them, and re-layouts: 6.54 us -> none
    pallas_call x1, Pallas kernels: 86.2 us -> 81.4 us  [on_device(): pl.pallas_call(functools.partial(kernel, nz, ndest), out_shape=[jax.Shape...]
    pallas_call x0 -> x1, Pallas kernels: none -> 1.41 us  [on_device(): pl.pallas_call(put_out, out_shape=[jax.ShapeDtypeStruct(o.shape, F32) for...]
where the time goes in v2:
time: 83.7 us; the launch traced here: 83.4 us
  Pallas kernels  82.8 us (99%)
    pallas_call x1, Pallas kernels, on_device(): pl.pallas_call(functools.partial(kernel, nz, ndest), out_shape=[jax.Shape...  81.4 us

profile of v2, /device:TPU:0, one launch (start us, length us, event | category | flops | bytes accessed | tf_op | source)
XLA Modules:
  0.0 83.4 jit_solution(15357650878555423701)
XLA Ops:
  0.6 81.4 %shard_map.84 = (f32[24,32]{1,0:T(8,128)}, f32[32,32]{1,0:T(8,128)}, f32[32,48]{1,0:T(8,128)}, f32[1,32]{1,0:T(1,128)}) custom-call(s32[24,48,256]{2,1,0:T(8,128)} %counts_in.1, f32[24,32]{1,0:T(8,128)} %anchor_in.1, f32[32,32]{1,0:T(8,128)} %dest_in.1, f32[32,48]{1,0:T(8,128)} %bitcast.4, f32[1,32]{1,0:T(1,128)} %bitcast.5), custom_call_target="tpu_custom_call" | custom-call | tf_op jit(solution)/shard_map/pallas_call | solution.py:364
  82.0 1.4 %shard_map.85 = (f32[24,32]{1,0:T(8,128)}, f32[32,32]{1,0:T(8,128)}, f32[32,48]{1,0:T(8,128)}, f32[1,32]{1,0:T(1,128)}) custom-call(f32[24,32]{1,0:T(8,128)} %get-tuple-element.12.refs_0_, f32[32,32]{1,0:T(8,128)} %get-tuple-element.13.refs_1_, f32[32,48]{1,0:T(8,128)} %get-tuple-element.14.refs_2_, f32[1,32]{1,0:T(1,128)} %get-tuple-element.15.refs_3_), custom_call_target="tpu_custom_call" | custom-call | tf_op jit(solution)/shard_map/pallas_call | solution.py:399

commit v3 on v2

--- a/solution.py
+++ b/solution.py
@@ -42,13 +42,11 @@
     chunks = vals.shape[1] // (8 * nhour)
     crow = 8 * nhour
 
-    def xpeer(t):
+    xpeers = []
+    for t in range(1, nx):
         idx = (xi + t) % nx
-        return idx, {"orig": zi * 2 + idx % 2, "dest": idx // 2}
-
-    def zpeer(t):
-        idx = (zi + t) % nz
-        return idx, {"orig": idx * 2 + core}
+        xpeers.append({"orig": zi * 2 + idx % 2, "dest": idx // 2})
+    zpeers = [{"orig": (zi + t) % nz * 2 + core} for t in range(1, nz)]
 
     small = [pltpu.make_async_copy(a, b, in_sem.at[q]) for q, (a, b) in enumerate(
         ((anchor_in, anchor_ref), (dest_in, dest_ref), (hour_in, hour_ref), (weight_in, weight_ref)))]
@@ -57,33 +55,24 @@
     for dma in small + large:
         dma.start()
     barrier = pltpu.get_barrier_semaphore()
-    for t in range(1, nx):
-        pl.semaphore_signal(barrier, inc=1, device_id=xpeer(t)[1], device_id_type=MESH)
-    for t in range(1, nz):
-        pl.semaphore_signal(barrier, inc=1, device_id=zpeer(t)[1], device_id_type=MESH)
-
-    def copy(ref, mine, theirs, send, recv, t, who):
-        return pltpu.make_async_remote_copy(
-            src_ref=ref.at[mine], dst_ref=ref.at[mine] if theirs is None else ref.at[theirs],
-            send_sem=send.at[t - 1], recv_sem=recv.at[mine if theirs is None else theirs],
-            device_id=who, device_id_type=MESH)
-
-    def start(ref, send, recv, peer, n, me):
-        for t in range(1, n):
-            copy(ref, me, None, send, recv, t, peer(t)[1]).start()
-
-    def collect(ref, send, recv, peer, n, me):
-        for t in range(1, n):
-            idx, who = peer(t)
-            copy(ref, idx, None, send, recv, t, who).wait_recv()
+    for who in zpeers + xpeers:
+        pl.semaphore_signal(barrier, inc=1, device_id=who, device_id_type=MESH)
+
+    def start(ref, send, recv, peers, me):
+        for who in peers:
+            pltpu.make_async_remote_copy(
+                src_ref=ref.at[me], dst_ref=ref.at[me], send_sem=send, recv_sem=recv,
+                device_id=who, device_id_type=MESH).start()
+
+    def wait_bytes(ref, sem):
+        pltpu.make_async_copy(ref, ref, sem).wait()
+
+    def collect(ref, recv, n):
+        wait_bytes(ref.at[pl.ds(0, n - 1)], recv)
         total = ref[0]
         for s in range(1, n):
             total = total + ref[s]
         return total
-
-    def finish(ref, send, recv, peer, n, me):
-        for t in range(1, n):
-            copy(ref, me, None, send, recv, t, peer(t)[1]).wait_send()
 
     lane = iota((1, LANES), 1)
     group = lane // rank
@@ -169,7 +158,7 @@
 
     pl.semaphore_wait(barrier, nx - 1 + nz - 1)
 
-    start(zbuf.at[0], z_send.at[0], z_recv.at[0], zpeer, nz, zi)
+    start(zbuf.at[0], z_send.at[0], z_recv.at[0], zpeers, zi)
 
     def acopy(slot):
         return pltpu.make_async_remote_copy(
@@ -207,11 +196,11 @@
 
     def ratio_chunk(s):
         left = ucur[8 * s:8 * s + 8]
+        rows = slice(s * crow, (s + 1) * crow)
         kh = (left[:, None, :] * ccur[...][None, :, :]).reshape(crow, 2 * LANES)
         hi = kh.astype(BF16).astype(F32)
         khs = jnp.where(high_lane, hi, kh - hi).astype(BF16)
         model = jnp.dot(khs, bmod[...], preferred_element_type=F32)
-        rows = slice(s * crow, (s + 1) * crow)
         values = jnp.concatenate([vals[0, rows], vals[1, rows]], axis=1)
         ratio = values / model
         rh = ratio.astype(BF16)
@@ -253,7 +242,7 @@
 
     acopy(1 - core).wait_recv()
     ucur[...] = jnp.concatenate([abuf[0], abuf[1]], axis=1)
-    gathered = collect(zbuf.at[0], z_send.at[0], z_recv.at[0], zpeer, nz, zi)
+    gathered = collect(zbuf.at[0], z_recv.at[0], nz)
     tcur[...] = gathered[:rank]
     set_right(tcur[...])
     for s in range(chunks):
@@ -265,8 +254,8 @@
             e = outer * 4 + inner
             xb, xs, xr = xbuf.at[e], x_send.at[e], x_recv.at[e]
             xb[xi] = pack_anchor(anchor_phi())
-            start(xb, xs, xr, xpeer, nx, xi)
-            s = collect(xb, xs, xr, xpeer, nx, xi)
+            start(xb, xs, xr, xpeers, xi)
+            s = collect(xb, xr, nx)
             ucur[...] = ucur[...] * (unpack_anchor(s) / (nhour * total_cols))
         col = jnp.sum(ucur[...], axis=0, keepdims=True)
         col = col[:, :LANES] + col[:, LANES:]
@@ -275,8 +264,8 @@
             e = 1 + outer * 2 + inner
             zb, zs, zr = zbuf.at[e], z_send.at[e], z_recv.at[e]
             zb[zi] = jnp.concatenate([dest_phi(), jnp.broadcast_to(col, (8, LANES))], axis=0)
-            start(zb, zs, zr, zpeer, nz, zi)
-            s = collect(zb, zs, zr, zpeer, nz, zi)
+            start(zb, zs, zr, zpeers, zi)
+            s = collect(zb, zr, nz)
             growth = tcur[...] * (s[:rank] / (total_rows * nhour))
             if inner == 0:
                 anchor_w = s[rank:rank + 1] / total_rows
@@ -290,15 +279,15 @@
             e = outer * 4 + 2 + inner
             xb, xs, xr = xbuf.at[e], x_send.at[e], x_recv.at[e]
             xb[xi] = pack_hour(hour_phi(), dest_col)
-            start(xb, xs, xr, xpeer, nx, xi)
-            s = collect(xb, xs, xr, xpeer, nx, xi)
+            start(xb, xs, xr, xpeers, xi)
+            s = collect(xb, xr, nx)
             h = outer * 2 + inner
             hb, hs, hr = hbuf.at[h], h_send.at[h], h_recv.at[h]
             hb[zi] = s
-            start(hb, hs, hr, zpeer, nz, zi)
+            start(hb, hs, hr, zpeers, zi)
             if inner == 0:
                 dest_w = spread_group(s[:1], copies - 1) / total_cols
-            s = collect(hb, hs, hr, zpeer, nz, zi)
+            s = collect(hb, hr, nz)
             growth = ccur[:, :LANES] * (unpack_hour(s) / (total_rows * total_cols))
             if inner == 0:
                 growth = growth / dest_w
@@ -325,16 +314,12 @@
     acopy(core).wait_send()
     for s in range(chunks):
         vcopy(s, core).wait_send()
-    finish(zbuf.at[0], z_send.at[0], z_recv.at[0], zpeer, nz, zi)
-
-    @pl.loop(0, OUTER * 4)
-    def _(e):
-        finish(xbuf.at[e], x_send.at[e], x_recv.at[e], xpeer, nx, xi)
-
-    @pl.loop(0, OUTER * 2)
-    def _(e):
-        finish(zbuf.at[1 + e], z_send.at[1 + e], z_recv.at[1 + e], zpeer, nz, zi)
-        finish(hbuf.at[e], h_send.at[e], h_recv.at[e], zpeer, nz, zi)
+    for e in range(OUTER * 4):
+        wait_bytes(xbuf.at[e, pl.ds(0, nx - 1)], x_send.at[e])
+    for e in range(1 + OUTER * 2):
+        wait_bytes(zbuf.at[e, pl.ds(0, nz - 1)], z_send.at[e])
+    for e in range(OUTER * 2):
+        wait_bytes(hbuf.at[e, pl.ds(0, nz - 1)], h_send.at[e])
 
 
 def put_out(*refs):
@@ -388,9 +373,9 @@
             vmem(dest_factor.shape, F32),
             vmem((rank, nhour), F32),
             vmem((1, rank), F32),
-            dma((OUTER * 4, nx - 1)), dma((OUTER * 4, nx)),
-            dma((1 + OUTER * 2, nz - 1)), dma((1 + OUTER * 2, nz)),
-            dma((OUTER * 2, nz - 1)), dma((OUTER * 2, nz)),
+            dma((OUTER * 4,)), dma((OUTER * 4,)),
+            dma((1 + OUTER * 2,)), dma((1 + OUTER * 2,)),
+            dma((OUTER * 2,)), dma((OUTER * 2,)),
             dma((chunks,)), dma((chunks,)), dma((2,)), dma((4 + chunks,)),
         ],
         compiler_params=pltpu.CompilerParams(

time: 83.7 us -> 82.3 us (0.983)
  Pallas kernels: 82.8 us -> 81.3 us
    pallas_call x1, Pallas kernels: 81.4 us -> 79.9 us  [on_device(): pl.pallas_call(functools.partial(kernel, nz, ndest), out_shape=[jax.Shape...]
where the time goes in v3:
time: 82.3 us; the launch traced here: 82 us
  Pallas kernels  81.3 us (99%)
    pallas_call x1, Pallas kernels, on_device(): pl.pallas_call(functools.partial(kernel, nz, ndest), out_shape=[jax.Shape...  79.9 us

profile of v3, /device:TPU:0, one launch (start us, length us, event | category | flops | bytes accessed | tf_op | source)
XLA Modules:
  0.0 82.0 jit_solution(3235937328690666667)
XLA Ops:
  0.6 79.9 %shard_map.84 = (f32[24,32]{1,0:T(8,128)}, f32[32,32]{1,0:T(8,128)}, f32[32,48]{1,0:T(8,128)}, f32[1,32]{1,0:T(1,128)}) custom-call(s32[24,48,256]{2,1,0:T(8,128)} %counts_in.1, f32[24,32]{1,0:T(8,128)} %anchor_in.1, f32[32,32]{1,0:T(8,128)} %dest_in.1, f32[32,48]{1,0:T(8,128)} %bitcast.4, f32[1,32]{1,0:T(1,128)} %bitcast.5), custom_call_target="tpu_custom_call" | custom-call | tf_op jit(solution)/shard_map/pallas_call | solution.py:349
  80.6 1.4 %shard_map.85 = (f32[24,32]{1,0:T(8,128)}, f32[32,32]{1,0:T(8,128)}, f32[32,48]{1,0:T(8,128)}, f32[1,32]{1,0:T(1,128)}) custom-call(f32[24,32]{1,0:T(8,128)} %get-tuple-element.12.refs_0_, f32[32,32]{1,0:T(8,128)} %get-tuple-element.13.refs_1_, f32[32,48]{1,0:T(8,128)} %get-tuple-element.14.refs_2_, f32[1,32]{1,0:T(1,128)} %get-tuple-element.15.refs_3_), custom_call_target="tpu_custom_call" | custom-call | tf_op jit(solution)/shard_map/pallas_call | solution.py:384

commit v4 on v3

--- a/solution.py
+++ b/solution.py
@@ -23,8 +23,8 @@
 def kernel(nz, ndest, counts_in, anchor_in, dest_in, hour_in, weight_in,
            anchor_out, dest_out, hour_out, weight_out,
            vals, outbox, ucur, ccur, tcur, bmod, balo,
-           xbuf, zbuf, hbuf, abuf, counts_ref, anchor_ref, dest_ref, hour_ref, weight_ref,
-           x_send, x_recv, z_send, z_recv, h_send, h_recv, v_send, v_recv, a_sem, in_sem):
+           ubuf, xbuf, zbuf, hbuf, abuf, counts_ref, anchor_ref, dest_ref, hour_ref, weight_ref,
+           u_send, u_recv, x_send, x_recv, z_send, z_recv, h_send, h_recv, v_send, v_recv, a_sem, in_sem):
     nrow, nhour, ncol = counts_ref.shape
     rank = hour_ref.shape[0]
     piece = dest_ref.shape[0]
@@ -102,7 +102,6 @@
 
     hrow = -(-nhour // (8 * (copies - 1))) * 8
     hblocks = nhour // hrow
-    ablocks = nrow // 8
 
     def pack_hour(p, extra):
         out = jnp.broadcast_to(extra, (hrow, LANES))
@@ -112,22 +111,6 @@
 
     def unpack_hour(s):
         return jnp.concatenate([spread_group(s, b) for b in range(hblocks)], axis=0)
-
-    def pack_anchor(p):
-        sides = []
-        for g in range(2):
-            side = p[:8, g * LANES:(g + 1) * LANES]
-            for b in range(1, ablocks):
-                side = jnp.where(group == b, p[8 * b:8 * b + 8, g * LANES:(g + 1) * LANES], side)
-            sides.append(side)
-        return jnp.concatenate(sides, axis=0)
-
-    def unpack_anchor(s):
-        sides = []
-        for g in range(2):
-            part = s[8 * g:8 * g + 8]
-            sides.append(jnp.concatenate([spread_group(part, b) for b in range(ablocks)], axis=0))
-        return jnp.concatenate(sides, axis=1)
 
     dst = iota((ncol, ncol), 1)
     src = iota((ncol, ncol), 0)
@@ -211,13 +194,22 @@
         return lax.dot_general(jnp.concatenate([rh, rl], axis=1), balo[...], (((1,), (1,)), ((), ())),
                                preferred_element_type=F32).reshape(8, nhour, LANES)
 
-    def anchor_phi():
-        parts = []
+    def anchor_step(e, before):
         for s in range(chunks):
+            before(s)
             left, khs, rh, rl = ratio_chunk(s)
-            parts.append(jnp.sum(along_of(rh, rl) * ccur[:, :LANES][None, :, :], axis=1))
-        p = pair_up(jnp.concatenate(parts, axis=0))
-        return jnp.concatenate([spread_group(p, 1), spread_group(p, 3)], axis=1)
+            p = pair_up(jnp.sum(along_of(rh, rl) * ccur[:, :LANES][None, :, :], axis=1))
+            ub = ubuf.at[e * chunks + s]
+            ub[xi] = p
+            start(ub, u_send.at[e * chunks + s], u_recv.at[e * chunks + s], xpeers, xi)
+
+    def anchor_update(e):
+        def update(s):
+            p = collect(ubuf.at[e * chunks + s], u_recv.at[e * chunks + s], nx)
+            p = jnp.concatenate([spread_group(p, 1), spread_group(p, 3)], axis=1)
+            rows = slice(8 * s, 8 * s + 8)
+            ucur[rows] = ucur[rows] * (p / (nhour * total_cols))
+        return update
 
     def hour_phi():
         p = None
@@ -228,10 +220,11 @@
             p = part if p is None else p + part
         return pair_up(p + pltpu.roll(p, 2 * rank, 1))
 
-    def dest_phi():
+    def dest_phi(before):
         dims = (((0,), (0,)), ((), ()))
         total = None
         for s in range(chunks):
+            before(s)
             left, khs, rh, rl = ratio_chunk(s)
             for g in range(2):
                 lanes = slice(g * LANES, (g + 1) * LANES)
@@ -250,20 +243,19 @@
 
     @pl.loop(0, OUTER)
     def _(outer):
+        before = lambda s: None
         for inner in range(INNER):
-            e = outer * 4 + inner
-            xb, xs, xr = xbuf.at[e], x_send.at[e], x_recv.at[e]
-            xb[xi] = pack_anchor(anchor_phi())
-            start(xb, xs, xr, xpeers, xi)
-            s = collect(xb, xr, nx)
-            ucur[...] = ucur[...] * (unpack_anchor(s) / (nhour * total_cols))
-        col = jnp.sum(ucur[...], axis=0, keepdims=True)
-        col = col[:, :LANES] + col[:, LANES:]
+            anchor_step(outer * INNER + inner, before)
+            before = anchor_update(outer * INNER + inner)
         anchor_w = None
         for inner in range(INNER):
             e = 1 + outer * 2 + inner
             zb, zs, zr = zbuf.at[e], z_send.at[e], z_recv.at[e]
-            zb[zi] = jnp.concatenate([dest_phi(), jnp.broadcast_to(col, (8, LANES))], axis=0)
+            p = dest_phi(before)
+            before = lambda s: None
+            col = jnp.sum(ucur[...], axis=0, keepdims=True)
+            col = col[:, :LANES] + col[:, LANES:]
+            zb[zi] = jnp.concatenate([p, jnp.broadcast_to(col, (8, LANES))], axis=0)
             start(zb, zs, zr, zpeers, zi)
             s = collect(zb, zr, nz)
             growth = tcur[...] * (s[:rank] / (total_rows * nhour))
@@ -276,7 +268,7 @@
         dest_col = to_row(jnp.sum(tcur[...], axis=1, keepdims=True))
         dest_w = None
         for inner in range(INNER):
-            e = outer * 4 + 2 + inner
+            e = outer * 2 + inner
             xb, xs, xr = xbuf.at[e], x_send.at[e], x_recv.at[e]
             xb[xi] = pack_hour(hour_phi(), dest_col)
             start(xb, xs, xr, xpeers, xi)
@@ -314,7 +306,9 @@
     acopy(core).wait_send()
     for s in range(chunks):
         vcopy(s, core).wait_send()
-    for e in range(OUTER * 4):
+    for e in range(OUTER * INNER * chunks):
+        wait_bytes(ubuf.at[e, pl.ds(0, nx - 1)], u_send.at[e])
+    for e in range(OUTER * 2):
         wait_bytes(xbuf.at[e, pl.ds(0, nx - 1)], x_send.at[e])
     for e in range(1 + OUTER * 2):
         wait_bytes(zbuf.at[e, pl.ds(0, nz - 1)], z_send.at[e])
@@ -364,7 +358,8 @@
             vmem((rank, LANES), F32),
             vmem((2 * LANES, 2 * LANES), BF16),
             vmem((4 * rank, 4 * LANES), BF16),
-            vmem((OUTER * 4, nx, hrow, LANES), F32),
+            vmem((OUTER * INNER * chunks, nx, 8, LANES), F32),
+            vmem((OUTER * 2, nx, hrow, LANES), F32),
             vmem((1 + OUTER * 2, nz, rank + 8, LANES), F32),
             vmem((OUTER * 2, nz, hrow, LANES), F32),
             vmem((2, nrow, LANES), F32),
@@ -373,7 +368,8 @@
             vmem(dest_factor.shape, F32),
             vmem((rank, nhour), F32),
             vmem((1, rank), F32),
-            dma((OUTER * 4,)), dma((OUTER * 4,)),
+            dma((OUTER * INNER * chunks,)), dma((OUTER * INNER * chunks,)),
+            dma((OUTER * 2,)), dma((OUTER * 2,)),
             dma((1 + OUTER * 2,)), dma((1 + OUTER * 2,)),
             dma((OUTER * 2,)), dma((OUTER * 2,)),
             dma((chunks,)), dma((chunks,)), dma((2,)), dma((4 + chunks,)),

time: 82.3 us -> 81.8 us (level)
  no operation moved by 1% of the time
where the time goes in v4:
time: 81.8 us; the launch traced here: 81.5 us
  Pallas kernels  80.9 us (99%)
    pallas_call x1, Pallas kernels, on_device(): pl.pallas_call(functools.partial(kernel, nz, ndest), out_shape=[jax.Shape...  79.5 us

profile of v4, /device:TPU:0, one launch (start us, length us, event | category | flops | bytes accessed | tf_op | source)
XLA Modules:
  0.0 81.5 jit_solution(12437001438935716534)
XLA Ops:
  0.6 79.5 %shard_map.84 = (f32[24,32]{1,0:T(8,128)}, f32[32,32]{1,0:T(8,128)}, f32[32,48]{1,0:T(8,128)}, f32[1,32]{1,0:T(1,128)}) custom-call(s32[24,48,256]{2,1,0:T(8,128)} %counts_in.1, f32[24,32]{1,0:T(8,128)} %anchor_in.1, f32[32,32]{1,0:T(8,128)} %dest_in.1, f32[32,48]{1,0:T(8,128)} %bitcast.4, f32[1,32]{1,0:T(1,128)} %bitcast.5), custom_call_target="tpu_custom_call" | custom-call | tf_op jit(solution)/shard_map/pallas_call | solution.py:343
  80.1 1.4 %shard_map.85 = (f32[24,32]{1,0:T(8,128)}, f32[32,32]{1,0:T(8,128)}, f32[32,48]{1,0:T(8,128)}, f32[1,32]{1,0:T(1,128)}) custom-call(f32[24,32]{1,0:T(8,128)} %get-tuple-element.12.refs_0_, f32[32,32]{1,0:T(8,128)} %get-tuple-element.13.refs_1_, f32[32,48]{1,0:T(8,128)} %get-tuple-element.14.refs_2_, f32[1,32]{1,0:T(1,128)} %get-tuple-element.15.refs_3_), custom_call_target="tpu_custom_call" | custom-call | tf_op jit(solution)/shard_map/pallas_call | solution.py:380
